TPU v7x, 768 devices: a whole 4x8x12 slice. The times are simulated.
768 devices in a mesh: row: 16 (over z_hi, x, core), col: 48 (over z_lo, y).
Axes of the slice: x: 4, y: 8, z: 12 (z_hi: 2, z_lo: 6; z = z_hi * 6 + z_lo), core: 2. Of those that a mesh axis runs over, the one named last changes fastest.
Arguments:
- amplitudes: float32 [24576, 24576], P('row', 'col'), may hold values from -6 to 6
- intermediates: float32 [1152, 24576], P('row', 'col'), may hold values from -0.078125 to 0.078125
- integrals: float32 [24576, 1152], P(('row', 'col')), may hold values from -6 to 6
- row_pairs: int32 [2, 24576], P(None, ('row', 'col')), may hold values from 0 to 383, as said below
- window_virtuals: int32 [18], replicated, may hold values from 0 to 383, as said below
- occupied_energies: float32 [64], replicated, may hold values from -2 to -0.3
- virtual_energies: float32 [384], replicated, may hold values from 0.5 to 3
Outputs:
- update: float32 [24576, 1152], P(('row', 'col'))
Inputs may be any that keep to these rules, and one draw needn't show every extreme that they name: `row_pairs`: every pair (a, i) with a < 384 and i < 64 stands in exactly one column. `window_virtuals`: 18 distinct virtual orbitals.
All inputs are finite; a program needn't handle non-finite values.
Results may differ from a plain program's by a relative error of at most 0.000062.
Values sent between devices are 32-bit elements; how exact they have to be, the bound alone decides.
A program may use at most 64 MiB of HBM per device.

v0:
```python
import jax
import jax.numpy as jnp
from jax import lax
from jax.sharding import PartitionSpec as P


def lookup_table(indices, table):
    positions = lax.broadcasted_iota(jnp.int32, (indices.shape[0], table.shape[0]), 1)
    matches = indices[:, None] == positions
    return jnp.sum(jnp.where(matches, table[None, :], jnp.float32(0.0)), axis=1)


def block_product(block_rows, gathered):
    return lax.dot_general(
        block_rows,
        gathered,
        (((1,), (1,)), ((), ())),
        precision=lax.Precision.HIGHEST,
        preferred_element_type=jnp.float32,
    )


def on_device(
    amplitudes,
    intermediates,
    integrals,
    row_pairs,
    window_virtuals,
    occupied_energies,
    virtual_energies,
):
    gathered = lax.all_gather(intermediates, "row", axis=0, tiled=True)
    cycle_term = lax.psum_scatter(
        block_product(amplitudes, gathered), "col", scatter_dimension=0, tiled=True
    )
    gap_row = lookup_table(row_pairs[0], virtual_energies) - lookup_table(
        row_pairs[1], occupied_energies
    )
    window_energy = lookup_table(window_virtuals, virtual_energies)
    gap_col = (window_energy[:, None] - occupied_energies[None, :]).reshape(-1)
    return (integrals + cycle_term) / (gap_row[:, None] + gap_col[None, :])


def solution(mesh):
    in_specs = (
        P("row", "col"),
        P("row", "col"),
        P(("row", "col"), None),
        P(None, ("row", "col")),
        P(),
        P(),
        P(),
    )
    out_specs = P(("row", "col"), None)
    return jax.shard_map(
        on_device, mesh=mesh, in_specs=in_specs, out_specs=out_specs, check_vma=False
    )
```

profile of v0, /device:TPU:4, one launch (start us, length us, event | category | flops | bytes accessed | tf_op | source)
XLA Modules:
  0.0 446.4 jit_solution(7039681441764809080)
XLA Ops:
  6.5 0.0 copy-start
  6.5 0.0 all-gather.2.cloned.1.call-start
  6.5 0.7 all-gather.2.cloned.1.call-update
  7.3 0.0 reduce-scatter.2.cloned.1.call-start
  7.3 95.6 %all-gather.2.cloned.1.call-done = f32[1152,512]{1,0:T(8,128)} async-done(((f32[72,512]{1,0:T(8,128)}), f32[1152,512]{1,0:T(8,128)}) %all-gather.2.cloned.1.call-update) | async-done | bytes 2359312 | tf_op jit(solution)/shard_map/all_gather | solution.py:32
  102.9 0.0 copy-done
  102.9 16.3 %fusion = f32[1536,1152]{1,0:T(8,128)} fusion(f32[1536,512]{1,0:T(8,128)S(1)} %copy-done, f32[1152,512]{1,0:T(8,128)} %all-gather.2.cloned.1.call-done), kind=kOutput, calls=%fused_computation.10 | convolution fusion | flops 10871635968 | bytes 12582912 | tf_op jit(solution)/shard_map/dot_general | solution.py:14
  119.2 0.0 copy-start.2
  119.2 0.0 copy-start.4
  119.2 0.0 copy-start.5
  119.2 0.0 copy-start.3
  119.2 0.0 copy-start.1
  119.3 0.0 reduce-scatter.2.cloned.1.call-update
  119.3 0.6 copy-done.2
  119.9 0.0 copy-done.4
  119.9 0.2 select_reduce_fusion.1
  120.1 0.0 copy-done.5
  120.1 0.1 broadcast_subtract_fusion
  120.2 0.1 sub.31
  120.2 0.0 copy-done.3
  120.2 0.2 select_reduce_fusion.2
  120.4 0.2 select_reduce_fusion
  120.6 317.2 %reduce-scatter.2.cloned.1.call-done = f32[32,1152]{1,0:T(8,128)} async-done(((f32[1536,1152]{1,0:T(8,128)}), f32[32,1152]{1,0:T(8,128)}) %reduce-scatter.2.cloned.1.call-update) | async-done | bytes 147472 | tf_op jit(solution)/shard_map/reduce_scatter | solution.py:33
  437.9 0.0 copy-done.1
  437.9 1.7 add_divide_fusion
  (2 shorter events, 0.0 us)
Async XLA Ops:
  6.5 96.4 %copy-start = (f32[1536,512]{1,0:T(8,128)S(1)}, f32[1536,512]{1,0:T(8,128)}, u32[]{:S(2)}) copy-start(f32[1536,512]{1,0:T(8,128)} %param.7) | copy-start | bytes 9437188
  6.5 96.4 %all-gather.2.cloned.1.call-start = ((), (), s32[]{:S(2)}) async-start(), calls=%async_computation.1 | async-start | bytes 2506752 | tf_op jit(solution)/shard_map/all_gather | solution.py:32
  7.3 430.6 %reduce-scatter.2.cloned.1.call-start = ((), (), s32[]{:S(2)}) async-start(), calls=%async_computation.2 | async-start | bytes 7225344 | tf_op jit(solution)/shard_map/reduce_scatter | solution.py:33
  119.2 0.7 copy-start.2
  119.2 0.7 copy-start.4
  119.2 0.9 copy-start.5
  119.2 1.0 copy-start.3
  119.2 318.6 %copy-start.1 = (f32[32,1152]{1,0:T(8,128)S(1)}, f32[32,1152]{1,0:T(8,128)}, u32[]{:S(2)}) copy-start(f32[32,1152]{1,0:T(8,128)} %param.9) | copy-start | bytes 442372
Sparse Core Ops, SparseCore 0:
  11.2 91.6 all-gather.1
  119.4 318.4 reduce-scatter.1
where the time goes:
time: 447 us; the launch traced here: 446 us
  waiting for transfers between devices  414 us (93%)
  matrix products  16.3 us (4%)
  between operations  13.4 us (3%)
    reduce_scatter x1, waiting for transfers between devices, on_device(): lax.psum_scatter(block_product(amplitudes, gathered), 'col', scatter_dime...  317 us
    all_gather x1, waiting for transfers between devices, on_device(): gathered = lax.all_gather(intermediates, 'row', axis=0, tiled=True)  95.6 us
    dot_general x1, matrix products, block_product(): lax.dot_general(block_rows, gathered, (((1,), (1,)), ((), ())), precision...  16.3 us
  transfers between devices with their start and end apart: 2, of which 2 were waited for; matrix products, arithmetic and copies ran while one was open for 0% of the time, Pallas kernels for 0%

commit v1 on v0

v1 whole, which is shorter than its diff:
```python
import functools

import jax
import jax.numpy as jnp
from jax import lax
from jax.experimental import pallas as pl
from jax.experimental.pallas import tpu as pltpu
from jax.sharding import PartitionSpec as P

MESH = pl.DeviceIdType.MESH
NX, NY, NZ, NL = 4, 8, 12, 6
RB = 32
DEPTH = 512
WIN = 72
CW = 384
NCOL = 1152


def lookup_table(indices, table):
    positions = lax.broadcasted_iota(jnp.int32, (indices.shape[0], table.shape[0]), 1)
    matches = indices[:, None] == positions
    return jnp.sum(jnp.where(matches, table[None, :], jnp.float32(0.0)), axis=1)


def split_hi_lo(value):
    hi = value.astype(jnp.bfloat16)
    return hi, (value - hi.astype(jnp.float32)).astype(jnp.bfloat16)


def kernel(
    a_hbm,
    b_ref,
    out_ref,
    a_vmem,
    a_hi,
    a_lo,
    gathered,
    relay,
    b_hi,
    b_lo,
    ybuf,
    ypart,
    zup,
    zdown,
    zpart,
    wup,
    wdown,
    usum,
    ubuf,
    a_sem,
    g_send,
    g_recv,
    y_send,
    y_recv,
    z_send,
    z_recv,
    w_send,
    w_recv,
    u_send,
    u_recv,
):
    row, col = lax.axis_index("row"), lax.axis_index("col")
    core = lax.rem(row, 2)
    x = lax.rem(lax.div(row, 2), NX)
    zhi = lax.div(row, 2 * NX)
    y = lax.rem(col, NY)
    i = lax.div(col, NY)
    z = zhi * NL + i
    sign = 1 - 2 * core

    def place(zhi_, x_, core_):
        return (zhi_ * NX + x_) * 2 + core_

    def device(x_, y_, z_, core_):
        return {
            "row": place(lax.div(z_, NL), x_, core_),
            "col": lax.rem(z_, NL) * NY + y_,
        }

    def at_x(step):
        return device(lax.rem(x + step + NX, NX), y, z, core)

    def at_y(step):
        return device(x, lax.rem(y + step + NY, NY), z, core)

    def at_z(step):
        return device(x, y, lax.rem(z + step + NZ, NZ), core)

    other_core = device(x, y, z, 1 - core)

    def remote(src, dst, send, recv, where):
        return pltpu.make_async_remote_copy(
            src_ref=src, dst_ref=dst, send_sem=send, recv_sem=recv,
            device_id=where, device_id_type=MESH,
        )

    a_copy = pltpu.make_async_copy(a_hbm, a_vmem, a_sem)
    a_copy.start()

    barrier = pltpu.get_barrier_semaphore()
    greeted = [at_x(1), at_x(-1), at_y(1), at_y(-1), at_z(1), at_z(-1), at_z(5), at_z(-5), other_core]
    for where in greeted:
        pl.semaphore_signal(barrier, inc=1, device_id=where, device_id_type=MESH)
    pl.semaphore_wait(barrier, len(greeted))

    sends = []

    def send(src, dst, send_index, recv_index, where):
        copy = remote(src, dst, g_send.at[send_index], g_recv.at[recv_index], where)
        copy.start()
        sends.append(copy)

    def wait_block(recv_index):
        remote(b_ref, relay, g_send.at[0], g_recv.at[recv_index], other_core).wait_recv()

    def x_of(step):
        return lax.rem(x + step + NX, NX)

    def spread(block, half_zhi, half):
        mine = gathered.at[place(half_zhi, x, core)]
        send(block, mine, 2 + 4 * half, 2 + 3 * half, at_x(sign))
        send(block, mine, 3 + 4 * half, 3 + 3 * half, at_x(-sign))
        send(block, mine, 10 + 4 * half, 8 + 4 * half, other_core)

    def collect(half_zhi, half):
        behind = gathered.at[place(half_zhi, x_of(-sign), core)]
        wait_block(2 + 3 * half)
        send(behind, behind, 4 + 4 * half, 4 + 3 * half, at_x(sign))
        send(behind, behind, 11 + 4 * half, 9 + 4 * half, other_core)
        ahead = gathered.at[place(half_zhi, x_of(sign), core)]
        wait_block(3 + 3 * half)
        send(ahead, ahead, 12 + 4 * half, 10 + 4 * half, other_core)

    def collect_far(half_zhi, half):
        far = gathered.at[place(half_zhi, x_of(2), core)]
        wait_block(4 + 3 * half)
        send(far, far, 13 + 4 * half, 11 + 4 * half, other_core)

    send(b_ref, relay, 0, 0, at_z(5 * sign))
    spread(b_ref, zhi, 0)
    gathered[row] = b_ref[...]

    a_copy.wait()

    @pl.loop(0, NL)
    def _(k):
        hi, lo = split_hi_lo(a_vmem[k])
        a_hi[k] = hi
        a_lo[k] = lo

    collect(zhi, 0)
    wait_block(0)
    next_zhi = lax.div(lax.rem(z + sign + NZ, NZ), NL)
    send(relay, gathered.at[place(1 - next_zhi, x, core)], 1, 1, at_z(sign))
    collect_far(zhi, 0)
    wait_block(1)
    spread(gathered.at[place(1 - zhi, x, core)], 1 - zhi, 1)
    collect(1 - zhi, 1)
    collect_far(1 - zhi, 1)
    for k in range(8):
        wait_block(8 + k)

    @pl.loop(0, 8)
    def _(k):
        value = gathered[pl.ds(2 * k, 2)].reshape(2 * WIN, DEPTH)
        hi, lo = split_hi_lo(value)
        rows = pl.ds(pl.multiple_of(2 * WIN * k, 2 * WIN), 2 * WIN)
        b_hi[rows] = hi
        b_lo[rows] = lo

    def product(hi, lo, first):
        bh, bl = b_hi[first : first + CW], b_lo[first : first + CW]

        def dot(p, q):
            return lax.dot_general(
                p, q, (((1,), (1,)), ((), ())), preferred_element_type=jnp.float32
            )

        return dot(hi, bh) + (dot(hi, bl) + dot(lo, bh))

    def y_product(direction, dest):
        hi = a_hi[:, dest].reshape(NL * RB, DEPTH)
        lo = a_lo[:, dest].reshape(NL * RB, DEPTH)
        return product(hi, lo, direction * CW).reshape(NL, RB, CW)

    def z_product(dest):
        hi = a_hi[dest].reshape(NY * RB, DEPTH)
        lo = a_lo[dest].reshape(NY * RB, DEPTH)
        return product(hi, lo, 2 * CW).reshape(NY, RB, CW)

    ypieces = [pl.ds(0, 3), pl.ds(3, 3)]
    zpieces = [pl.ds(0, 4), pl.ds(4, 4)]

    def y_copy(direction, slot, piece):
        part = ypieces[piece]
        return remote(
            ybuf.at[direction, slot, part], ybuf.at[direction, slot + 1, part],
            y_send.at[direction, slot, piece], y_recv.at[direction, slot, piece],
            at_y(1 - 2 * direction),
        )

    def z_copy(way, slot, piece):
        buf = (zup, zdown)[way]
        part = zpieces[piece]
        return remote(
            buf.at[slot, part], buf.at[slot, part],
            z_send.at[way, slot, piece], z_recv.at[way, slot, piece], at_z(1 - 2 * way),
        )

    def z_step(turn):
        for way in range(2):
            far = i if way == 0 else NL - 1 - i
            buf = (zup, zdown)[way]

            @pl.when(turn >= far)
            def _():
                slot = turn - far
                dest = NL - 1 - slot if way == 0 else slot

                @pl.when(far == 0)
                def _():
                    buf[slot] = z_product(dest)
                    for piece in range(2):
                        z_copy(way, slot, piece).start()

                @pl.when(far > 0)
                def _():
                    zpart[...] = z_product(dest)
                    for piece in range(2):
                        z_copy(way, slot, piece).wait_recv()
                        buf[slot, zpieces[piece]] += zpart[zpieces[piece]]
                        z_copy(way, slot, piece).start()

    for direction in range(2):
        dest = lax.rem(y - 1 + 2 * direction + NY, NY)
        ybuf[direction, 0] = y_product(direction, dest)
        for piece in range(2):
            y_copy(direction, 0, piece).start()
    z_step(0)

    @pl.loop(0, NY - 1)
    def _(r):
        for direction in range(2):
            dest = lax.rem(y + (2 + r) * (2 * direction - 1) + 2 * NY, NY)
            ypart[direction] = y_product(direction, dest)
        for piece in range(2):
            for direction in range(2):
                part = ypieces[piece]
                y_copy(direction, r, piece).wait_recv()
                ybuf[direction, r + 1, part] += ypart[direction, part]

                @pl.when(r < NY - 2)
                def _():
                    y_copy(direction, r + 1, piece).start()

        @pl.when((r < 2) | (r == 3) | (r == 4))
        def _():
            z_step(jnp.where(r < 2, r + 1, r))

    usum[...] = z_product(i)
    for way in range(2):
        far = i if way == 0 else NL - 1 - i
        buf = (zup, zdown)[way]

        @pl.when(far > 0)
        def _():
            slot = NL - 1 - far
            for piece in range(2):
                z_copy(way, slot, piece).wait_recv()
                usum[zpieces[piece]] += buf[slot, zpieces[piece]]

    def w_copy(way, slot):
        buf = (wup, wdown)[way]
        return remote(
            buf.at[slot], buf.at[slot], w_send.at[way, slot], w_recv.at[way, slot], at_z(1 - 2 * way)
        )

    def w_step(turn):
        for way in range(2):
            far = i if way == 0 else NL - 1 - i
            buf = (wup, wdown)[way]

            @pl.when(turn >= far)
            def _():
                slot = turn - far
                dest = NL - 1 - slot if way == 0 else slot

                @pl.when(far == 0)
                def _():
                    buf[slot] = ybuf[:, NY - 1, dest]

                @pl.when(far > 0)
                def _():
                    w_copy(way, slot).wait_recv()
                    buf[slot] += ybuf[:, NY - 1, dest]

                w_copy(way, slot).start()

    half = RB // 2

    def u_copy(direction, slot):
        return remote(
            ubuf.at[direction, slot], ubuf.at[direction, slot + 1],
            u_send.at[direction, slot], u_recv.at[direction, slot], at_y(1 - 2 * direction),
        )

    w_step(0)
    for direction in range(2):
        dest = lax.rem(y - 1 + 2 * direction + NY, NY)
        ubuf[direction, 0] = usum[dest, direction * half : (direction + 1) * half]
        u_copy(direction, 0).start()

    @pl.loop(0, NY - 1)
    def _(r):
        for direction in range(2):
            dest = lax.rem(y + (2 + r) * (2 * direction - 1) + 2 * NY, NY)
            u_copy(direction, r).wait_recv()
            ubuf[direction, r + 1] += usum[dest, direction * half : (direction + 1) * half]

            @pl.when(r < NY - 2)
            def _():
                u_copy(direction, r + 1).start()

        @pl.when((r == 1) | (r == 3) | (r == 4) | (r == 6))
        def _():
            w_step(jnp.where(r == 1, 1, jnp.where(r == 3, 2, jnp.where(r == 4, 3, 4))))

    for direction in range(2):
        out_ref[direction * half : (direction + 1) * half, 2 * CW :] = ubuf[direction, NY - 1]
        out_ref[:, direction * CW : (direction + 1) * CW] = ybuf[direction, NY - 1, i]
    for way in range(2):
        far = i if way == 0 else NL - 1 - i
        buf = (wup, wdown)[way]

        @pl.when(far > 0)
        def _():
            slot = NL - 1 - far
            w_copy(way, slot).wait_recv()
            for direction in range(2):
                out_ref[:, direction * CW : (direction + 1) * CW] += buf[slot, direction]

    for copy in sends:
        copy.wait_send()

    @pl.loop(0, NY - 1)
    def _(r):
        for direction in range(2):
            for piece in range(2):
                y_copy(direction, r, piece).wait_send()
            u_copy(direction, r).wait_send()

    @pl.loop(0, NL - 1)
    def _(slot):
        for way in range(2):
            far = i if way == 0 else NL - 1 - i

            @pl.when(slot < NL - 1 - far)
            def _():
                for piece in range(2):
                    z_copy(way, slot, piece).wait_send()
                w_copy(way, slot).wait_send()


def cycle_rows(amplitudes, intermediates):
    f32, bf16 = jnp.float32, jnp.bfloat16
    vmem, dma = pltpu.VMEM, pltpu.SemaphoreType.DMA
    return pl.pallas_call(
        kernel,
        out_shape=jax.ShapeDtypeStruct((RB, NCOL), f32),
        in_specs=[
            pl.BlockSpec(memory_space=pl.ANY),
            pl.BlockSpec(memory_space=pltpu.VMEM),
        ],
        out_specs=pl.BlockSpec(memory_space=pltpu.VMEM),
        scratch_shapes=[
            vmem((NL, NY, RB, DEPTH), f32),
            vmem((NL, NY, RB, DEPTH), bf16),
            vmem((NL, NY, RB, DEPTH), bf16),
            vmem((4 * NX, WIN, DEPTH), f32),
            vmem((WIN, DEPTH), f32),
            vmem((NCOL, DEPTH), bf16),
            vmem((NCOL, DEPTH), bf16),
            vmem((2, NY, NL, RB, CW), f32),
            vmem((2, NL, RB, CW), f32),
            vmem((NL - 1, NY, RB, CW), f32),
            vmem((NL - 1, NY, RB, CW), f32),
            vmem((NY, RB, CW), f32),
            vmem((NL - 1, 2, RB, CW), f32),
            vmem((NL - 1, 2, RB, CW), f32),
            vmem((NY, RB, CW), f32),
            vmem((2, NY, RB // 2, CW), f32),
            dma,
            dma((18,)),
            dma((16,)),
            dma((2, NY - 1, 2)),
            dma((2, NY - 1, 2)),
            dma((2, NL - 1, 2)),
            dma((2, NL - 1, 2)),
            dma((2, NL - 1)),
            dma((2, NL - 1)),
            dma((2, NY - 1)),
            dma((2, NY - 1)),
        ],
        compiler_params=pltpu.CompilerParams(
            collective_id=0, has_side_effects=True, vmem_limit_bytes=60 * 2**20
        ),
    )(amplitudes.reshape(NL, NY, RB, DEPTH), intermediates)


def on_device(
    amplitudes,
    intermediates,
    integrals,
    row_pairs,
    window_virtuals,
    occupied_energies,
    virtual_energies,
):
    cycle_term = cycle_rows(amplitudes, intermediates)
    gap_row = lookup_table(row_pairs[0], virtual_energies) - lookup_table(
        row_pairs[1], occupied_energies
    )
    window_energy = lookup_table(window_virtuals, virtual_energies)
    gap_col = (window_energy[:, None] - occupied_energies[None, :]).reshape(-1)
    return (integrals + cycle_term) / (gap_row[:, None] + gap_col[None, :])


def solution(mesh):
    in_specs = (
        P("row", "col"),
        P("row", "col"),
        P(("row", "col"), None),
        P(None, ("row", "col")),
        P(),
        P(),
        P(),
    )
    out_specs = P(("row", "col"), None)
    return jax.shard_map(
        on_device, mesh=mesh, in_specs=in_specs, out_specs=out_specs, check_vma=False
    )
```

time: 447 us -> 130 us (0.29)
  the two profiles are of different devices: /device:TPU:4 before, /device:TPU:8 now
where the time goes in v1:
time: 130 us
  Pallas kernels  124 us (95%)
  other arithmetic  5 us (4%)
    pallas_call x1, Pallas kernels, cycle_rows(): pl.pallas_call(kernel, out_shape=jax.ShapeDtypeStruct((RB, NCOL), f32), i...  124 us
    reduce_sum x3, other arithmetic, lookup_table(): return jnp.sum(jnp.where(matches, table[None, :], jnp.float32(0.0)), axis=1)  2.6 us

profile of v1, /device:TPU:8, one launch (start us, length us, event | category | flops | bytes accessed | tf_op | source)
XLA Modules:
  0.0 129.8 jit_solution(481732826202716543)
XLA Ops:
  0.0 0.0 copy-start
  0.0 0.9 select_reduce_fusion.1
  0.9 0.8 slice_bitcast_fusion
  1.7 0.8 select_reduce_fusion.2
  2.5 0.9 select_reduce_fusion
  3.4 0.7 broadcast_subtract_fusion
  4.1 0.1 sub.31
  4.2 123.9 %shard_map.73 = f32[32,1152]{1,0:T(8,128)} custom-call(f32[6,8,32,512]{3,2,1,0:T(8,128)} %bitcast.5, f32[72,512]{1,0:T(8,128)} %b_ref.1), custom_call_target="tpu_custom_call" | custom-call | tf_op jit(solution)/shard_map/pallas_call | solution.py:367
  128.1 0.0 copy-done
  128.1 1.7 %add_divide_fusion = f32[32,1152]{1,0:T(8,128)} fusion(f32[32,1152]{1,0:T(8,128)S(1)} %copy-done, f32[32,1152]{1,0:T(8,128)} %shard_map.73, f32[1152]{0:T(1024)S(1)} %sub.31, f32[32]{0:T(128)S(1)} %sub.27), kind=kLoop, calls=%fused_computation | loop fusion | flops 110592 | bytes 447104 | tf_op jit(solution)/shard_map/div | solution.py:425
  (1 shorter events, 0.0 us)
Async XLA Ops:
  0.0 128.1 %copy-start = (f32[32,1152]{1,0:T(8,128)S(1)}, f32[32,1152]{1,0:T(8,128)}, u32[]{:S(2)}) copy-start(f32[32,1152]{1,0:T(8,128)} %param.9) | copy-start | bytes 442372

commit v2 on v0

v2 whole, which is shorter than its diff:
```python
import jax
import jax.numpy as jnp
from jax import lax
from jax.experimental import pallas as pl
from jax.experimental.pallas import tpu as pltpu
from jax.sharding import PartitionSpec as P

MESH = pl.DeviceIdType.MESH
NX, NY, NZ, NL = 4, 8, 12, 6
RB = 32
DEPTH = 512
WIN = 72
HALF = 576
NCOL, NV, NO, NB = 1152, 384, 64, 18

Y_STREAMS = ((0, 256), (512, 512))
Z_STREAMS = ((256, 256), (1024, 128))
Y_PIECES = (3, 3)


def split_hi_lo(value):
    hi = value.astype(jnp.bfloat16)
    return hi, (value - hi.astype(jnp.float32)).astype(jnp.bfloat16)


def as_column(line):
    n = line.shape[1]
    here = lax.broadcasted_iota(jnp.int32, (n, n), 0) == lax.broadcasted_iota(jnp.int32, (n, n), 1)
    return jnp.sum(jnp.where(here, jnp.broadcast_to(line, (n, n)), jnp.zeros_like(line)), axis=1, keepdims=True)


def look_up(indices, table):
    n, m = indices.shape[0], table.shape[1]
    match = indices == lax.broadcasted_iota(jnp.int32, (n, m), 1)
    return jnp.sum(jnp.where(match, jnp.broadcast_to(table, (n, m)), 0.0), axis=1, keepdims=True)


def kernel(
    a_hbm, b_ref, integrals_hbm, pairs_ref, window_ref, occupied_ref, virtual_ref, out_ref,
    a_vmem, integrals, a_hi, a_lo, gathered, b_hi, b_lo, result,
    yc0, yc1, yb0, yb1, zc0, zc1, zup0, zup1, zdn0, zdn1,
    wup0, wup1, wdn0, wdn1, ub0, ub1,
    l_sem, g_send, g_recv, y_send0, y_recv0, y_send1, y_recv1, z_send, z_recv, w_send, w_recv, u_send, u_recv,
):
    ycs, ybs, y_sends, y_recvs = (yc0, yc1), (yb0, yb1), (y_send0, y_send1), (y_recv0, y_recv1)
    zcs, zbufs = (zc0, zc1), ((zup0, zdn0), (zup1, zdn1))
    wbufs, ubs = ((wup0, wdn0), (wup1, wdn1)), (ub0, ub1)

    row, col = lax.axis_index("row"), lax.axis_index("col")
    core = lax.rem(row, 2)
    x = lax.rem(lax.div(row, 2), NX)
    zhi = lax.div(row, 2 * NX)
    y = lax.rem(col, NY)
    i = lax.div(col, NY)
    z = zhi * NL + i
    sign = 1 - 2 * core

    def device(x_, y_, z_, core_):
        return {
            "row": (lax.div(z_, NL) * NX + x_) * 2 + core_,
            "col": lax.rem(z_, NL) * NY + y_,
        }

    def x_of(step):
        return lax.rem(x + step + NX, NX)

    def at_x(step):
        return device(x_of(step), y, z, core)

    def at_y(step):
        return device(x, lax.rem(y + step + NY, NY), z, core)

    def at_z(step):
        return device(x, y, lax.rem(z + step + NZ, NZ), core)

    other_core = device(x, y, z, 1 - core)

    def remote(src, dst, send, recv, where):
        return pltpu.make_async_remote_copy(
            src_ref=src, dst_ref=dst, send_sem=send, recv_sem=recv,
            device_id=where, device_id_type=MESH,
        )

    a_copy = pltpu.make_async_copy(a_hbm, a_vmem, l_sem.at[0])
    a_copy.start()
    i_copy = pltpu.make_async_copy(integrals_hbm, integrals, l_sem.at[1])
    i_copy.start()

    barrier = pltpu.get_barrier_semaphore()
    greeted = [at_x(1), at_x(-1), at_z(1), at_z(-1), at_z(6), other_core]
    greeted += [at_y(k) for k in range(1, NY)]
    for where in greeted:
        pl.semaphore_signal(barrier, inc=1, device_id=where, device_id_type=MESH)
    pl.semaphore_wait(barrier, len(greeted))

    events = []
    finish = []

    def event(when, do):
        events.append((when, len(events), do))

    def slot(half, x_, core_):
        return gathered.at[half, x_ * 2 + core_]

    def send(src, dst, send_index, recv_index, where):
        copy = remote(src, dst, g_send.at[send_index], g_recv.at[recv_index], where)
        copy.start()
        finish.append(copy.wait_send)

    def wait_block(recv_index):
        remote(b_ref, slot(0, x, core), g_send.at[0], g_recv.at[recv_index], other_core).wait_recv()

    def spread(block, half):
        mine = slot(half, x, core)
        send(block, mine, 1 + 7 * half, 1 + 7 * half, at_x(sign))
        send(block, mine, 2 + 7 * half, 2 + 7 * half, at_x(-sign))
        send(block, mine, 3 + 7 * half, 3 + 7 * half, other_core)

    def collect(half):
        behind = slot(half, x_of(-sign), core)
        wait_block(1 + 7 * half)
        send(behind, behind, 4 + 7 * half, 4 + 7 * half, at_x(sign))
        send(behind, behind, 5 + 7 * half, 5 + 7 * half, other_core)
        ahead = slot(half, x_of(sign), core)
        wait_block(2 + 7 * half)
        send(ahead, ahead, 6 + 7 * half, 6 + 7 * half, other_core)

    def collect_far(half):
        far = slot(half, x_of(2), core)
        wait_block(4 + 7 * half)
        send(far, far, 7 + 7 * half, 7 + 7 * half, other_core)

    def split_b(half):
        for k in (3, 5, 6, 7):
            wait_block(k + 7 * half)

        @pl.loop(0, 4)
        def _(k):
            hi, lo = split_hi_lo(gathered[half, pl.ds(2 * k, 2)].reshape(2 * WIN, DEPTH))
            rows = pl.ds(pl.multiple_of(HALF * half + 2 * WIN * k, 2 * WIN), 2 * WIN)
            b_hi[rows] = hi
            b_lo[rows] = lo

    def multiply(target, first, width):
        bh, bl = b_hi[first : first + width], b_lo[first : first + width]

        def dot(p, q):
            return lax.dot_general(
                p, q, (((1,), (1,)), ((), ())), preferred_element_type=jnp.float32
            )

        @pl.loop(0, NL)
        def _(k):
            hi = a_hi[k].reshape(NY * RB, DEPTH)
            lo = a_lo[k].reshape(NY * RB, DEPTH)
            value = dot(hi, bh) + (dot(hi, bl) + dot(lo, bh))
            target[k] = value.reshape(NY, RB, width)

    def y_rows(n, direction, piece):
        size = 3 // Y_PIECES[n]
        return pl.ds(3 * direction + piece * size, size)

    def y_dest(direction, step):
        return lax.rem(y + (1 + step) * (2 * direction - 1) + NY, NY)

    def y_copy(n, direction, step, piece):
        rows = y_rows(n, direction, piece)
        src = ycs[n].at[rows, y_dest(direction, 0)] if step == 0 else ybs[n].at[step - 1, rows]
        index = (direction, step, piece)
        return remote(
            src, ybs[n].at[step, rows], y_sends[n].at[index], y_recvs[n].at[index],
            at_y(1 - 2 * direction),
        )

    def y_start(n, piece):
        for direction in range(2):
            y_copy(n, direction, 0, piece).start()

    def y_step(n, step, piece):
        for direction in range(2):
            rows = y_rows(n, direction, piece)
            y_copy(n, direction, step, piece).wait_recv()
            ybs[n][step, rows] += ycs[n][rows, y_dest(direction, step + 1)]
            if step < NY - 2:
                y_copy(n, direction, step + 1, piece).start()

    def line(bufs, own, parts, sends, recvs, n):
        def copy(way, index, piece, src):
            part = parts[piece]
            return remote(
                src, bufs[way].at[index, part],
                sends.at[n, way, index, piece], recvs.at[n, way, index, piece], at_z(1 - 2 * way),
            )

        def turn(count):
            for way in range(2):
                far = i if way == 0 else NL - 1 - i
                index = count - far
                dest = NL - 1 - index if way == 0 else index

                @pl.when(far == 0)
                def _():
                    for piece in range(2):
                        copy(way, index, piece, own.at[dest, parts[piece]]).start()

                @pl.when((far > 0) & (far <= count))
                def _():
                    for piece in range(2):
                        part = parts[piece]
                        held = bufs[way].at[index, part]
                        copy(way, index, piece, held).wait_recv()
                        bufs[way][index, part] += own[dest, part]
                        copy(way, index, piece, held).start()

        def last():
            for way in range(2):
                far = i if way == 0 else NL - 1 - i
                index = NL - 1 - far

                @pl.when(far > 0)
                def _():
                    for piece in range(2):
                        part = parts[piece]
                        copy(way, index, piece, bufs[way].at[index, part]).wait_recv()
                        own[i, part] += bufs[way][index, part]

        def sent():
            for way in range(2):
                far = i if way == 0 else NL - 1 - i

                @pl.loop(0, NL - 1)
                def _(index):
                    @pl.when(index < NL - 1 - far)
                    def _():
                        for piece in range(2):
                            copy(way, index, piece, bufs[way].at[index, parts[piece]]).wait_send()

        finish.append(sent)
        return turn, last

    half_rows = [pl.ds(0, RB // 2), pl.ds(RB // 2, RB // 2)]
    half_y = [pl.ds(0, NY // 2), pl.ds(NY // 2, NY // 2)]
    z_lines = [line(zbufs[n], zcs[n], half_y, z_send, z_recv, n) for n in range(2)]
    w_lines = [line(wbufs[n], ybs[n].at[NY - 2], half_rows, w_send, w_recv, n) for n in range(2)]

    def u_copy(n, k):
        return remote(
            zcs[n].at[i, lax.rem(y + k, NY)], ubs[n].at[k - 1],
            u_send.at[n, k - 1], u_recv.at[n, k - 1], at_y(k),
        )

    def u_start(n):
        for k in (4, 3, 5, 2, 6, 1, 7):
            u_copy(n, k).start()

    def u_last(n):
        first, width = Z_STREAMS[n]
        total = zcs[n][i, y]
        for k in range(1, NY):
            u_copy(n, k).wait_recv()
            total = total + ubs[n][k - 1]
        result[:, first : first + width] = total

    def w_last(n):
        first, width = Y_STREAMS[n]
        w_lines[n][1]()
        result[:, first : first + width] = ybs[n][NY - 2, i]

    send(b_ref, slot(1, x, core), 0, 0, at_z(6))
    spread(b_ref, 0)
    gathered[0, x * 2 + core] = b_ref[...]
    a_copy.wait()

    @pl.loop(0, NL)
    def _(k):
        hi, lo = split_hi_lo(a_vmem[k])
        a_hi[k] = hi
        a_lo[k] = lo

    event(5.0, lambda: collect(0))
    event(8.5, lambda: collect_far(0))
    event(10.5, lambda: split_b(0))
    event(11.0, lambda: multiply(ycs[0], *Y_STREAMS[0]))
    for piece in range(Y_PIECES[0]):
        event(12.5, lambda piece=piece: y_start(0, piece))
    event(13.0, lambda: multiply(zcs[0], *Z_STREAMS[0]))
    event(14.0, lambda: z_lines[0][0](0))

    def pair():
        wait_block(0)
        spread(slot(1, x, core), 1)

    event(15.0, pair)
    event(20.0, lambda: collect(1))
    event(23.5, lambda: collect_far(1))
    event(26.0, lambda: split_b(1))
    event(26.5, lambda: multiply(ycs[1], *Y_STREAMS[1]))
    for piece in range(Y_PIECES[1]):
        event(30.0, lambda piece=piece: y_start(1, piece))
    event(30.2, lambda: multiply(zcs[1], *Z_STREAMS[1]))
    event(31.0, lambda: z_lines[1][0](0))
    for n, begin, period in ((0, 13.0, 2.6), (1, 30.0, 4.3)):
        for step in range(NY - 1):
            for piece in range(Y_PIECES[n]):
                when = begin + period * (step + (piece + 1) / Y_PIECES[n])
                event(when, lambda n=n, step=step, piece=piece: y_step(n, step, piece))
    for lines, n, begin, period in (
        (z_lines, 0, 15.0, 6.5), (z_lines, 1, 31.0, 6.5), (w_lines, 0, 32.0, 5.0), (w_lines, 1, 60.5, 2.6),
    ):
        for count in range(0 if lines is w_lines else 1, NL - 1):
            event(begin + period * count, lambda lines=lines, n=n, count=count: lines[n][0](count))
    event(47.5, z_lines[0][1])
    event(47.6, lambda: u_start(0))
    event(57.0, lambda: w_last(0))
    event(63.9, z_lines[1][1])
    event(64.0, lambda: u_start(1))
    event(72.0, lambda: u_last(0))
    event(72.1, lambda: u_last(1))
    event(73.5, lambda: w_last(1))
    for _, _, do in sorted(events, key=lambda e: e[:2]):
        do()

    i_copy.wait()
    pairs = pairs_ref[...]
    gap_row = look_up(as_column(pairs[0:1]), virtual_ref[...]) - look_up(as_column(pairs[1:2]), occupied_ref[...])
    energy = look_up(as_column(window_ref[...]), virtual_ref[...])
    block = lax.broadcasted_iota(jnp.int32, (NB, NCOL), 1) // NO == lax.broadcasted_iota(jnp.int32, (NB, NCOL), 0)
    energy = jnp.sum(jnp.where(block, jnp.broadcast_to(energy, (NB, NCOL)), 0.0), axis=0, keepdims=True)
    within = lax.broadcasted_iota(jnp.int32, (NO, NCOL), 1) % NO == lax.broadcasted_iota(jnp.int32, (NO, NCOL), 0)
    occupied = jnp.broadcast_to(as_column(occupied_ref[...]), (NO, NCOL))
    gap_col = energy - jnp.sum(jnp.where(within, occupied, 0.0), axis=0, keepdims=True)
    value = result[...]
    turned = jnp.concatenate([value[:, HALF:], value[:, :HALF]], axis=1)
    cycle_term = jnp.where(zhi == 0, value, turned)
    out_ref[...] = (integrals[...] + cycle_term) / (gap_row + gap_col)

    for wait in finish:
        wait()
    for n in range(2):
        for direction in range(2):
            for step in range(NY - 1):
                for piece in range(Y_PIECES[n]):
                    y_copy(n, direction, step, piece).wait_send()
        for k in range(1, NY):
            u_copy(n, k).wait_send()


def on_device(
    amplitudes, intermediates, integrals, row_pairs, window_virtuals, occupied_energies, virtual_energies
):
    f32, bf16 = jnp.float32, jnp.bfloat16
    vmem, dma = pltpu.VMEM, pltpu.SemaphoreType.DMA
    y_widths, z_widths = [w for _, w in Y_STREAMS], [w for _, w in Z_STREAMS]
    whole, away = pl.BlockSpec(memory_space=pltpu.VMEM), pl.BlockSpec(memory_space=pl.ANY)
    return pl.pallas_call(
        kernel,
        out_shape=jax.ShapeDtypeStruct((RB, NCOL), f32),
        in_specs=[away, whole, away, whole, whole, whole, whole],
        out_specs=whole,
        scratch_shapes=[
            vmem((NL, NY, RB, DEPTH), f32),
            vmem((RB, NCOL), f32),
            vmem((NL, NY, RB, DEPTH), bf16),
            vmem((NL, NY, RB, DEPTH), bf16),
            vmem((2, 2 * NX, WIN, DEPTH), f32),
            vmem((NCOL, DEPTH), bf16),
            vmem((NCOL, DEPTH), bf16),
            vmem((RB, NCOL), f32),
            *[vmem((NL, NY, RB, w), f32) for w in y_widths],
            *[vmem((NY - 1, NL, RB, w), f32) for w in y_widths],
            *[vmem((NL, NY, RB, w), f32) for w in z_widths],
            *[vmem((NL - 1, NY, RB, w), f32) for w in z_widths],
            *[vmem((NL - 1, NY, RB, w), f32) for w in z_widths],
            *[vmem((NL - 1, RB, w), f32) for w in y_widths],
            *[vmem((NL - 1, RB, w), f32) for w in y_widths],
            *[vmem((NY - 1, RB, w), f32) for w in z_widths],
            dma((2,)),
            dma((15,)),
            dma((15,)),
            dma((2, NY - 1, Y_PIECES[0])),
            dma((2, NY - 1, Y_PIECES[0])),
            dma((2, NY - 1, Y_PIECES[1])),
            dma((2, NY - 1, Y_PIECES[1])),
            dma((2, 2, NL - 1, 2)),
            dma((2, 2, NL - 1, 2)),
            dma((2, 2, NL - 1, 2)),
            dma((2, 2, NL - 1, 2)),
            dma((2, NY - 1)),
            dma((2, NY - 1)),
        ],
        compiler_params=pltpu.CompilerParams(
            collective_id=0, has_side_effects=True, vmem_limit_bytes=60 * 2**20
        ),
    )(
        amplitudes.reshape(NL, NY, RB, DEPTH), intermediates, integrals, row_pairs,
        window_virtuals.reshape(1, NB), occupied_energies.reshape(1, NO), virtual_energies.reshape(1, NV),
    )


def solution(mesh):
    in_specs = (
        P("row", "col"),
        P("row", "col"),
        P(("row", "col"), None),
        P(None, ("row", "col")),
        P(),
        P(),
        P(),
    )
    out_specs = P(("row", "col"), None)
    return jax.shard_map(
        on_device, mesh=mesh, in_specs=in_specs, out_specs=out_specs, check_vma=False
    )
```

time: 447 us -> 119 us (0.27)
  the two profiles are of different devices: /device:TPU:4 before, /device:TPU:2 now
where the time goes in v2:
time: 119 us
  Pallas kernels  116 us (97%)
  local copies, waits for them, and re-layouts  2.83 us (2%)
    pallas_call x1, Pallas kernels, on_device(): pl.pallas_call(kernel, out_shape=jax.ShapeDtypeStruct((RB, NCOL), f32), i...  116 us

profile of v2, /device:TPU:2, one launch (start us, length us, event | category | flops | bytes accessed | tf_op | source)
XLA Modules:
  0.0 118.6 jit_solution(9464163950962313076)
XLA Ops:
  0.0 1.2 %reshape.15.virtual_ref = f32[1,384]{1,0:T(1,128)} reshape(f32[384]{0:T(512)} %param.13) | data formatting | bytes 3072 | tf_op jit(solution)/shard_map/reshape | solution.py:396
  1.2 115.8 %shard_map.73 = f32[32,1152]{1,0:T(8,128)} custom-call(f32[6,8,32,512]{3,2,1,0:T(8,128)} %bitcast.3, f32[72,512]{1,0:T(8,128)} %b_ref.1, f32[32,1152]{1,0:T(8,128)} %integrals_hbm.1, s32[2,32]{1,0:T(2,128)} %pairs_ref.1, s32[1,18]{1,0:T(1,128)} %bitcast.4, f32[1,64]{1,0:T(1,128)} %bitcast.5, f32[1,384]{1,0:T(1,128)} %reshape.15.virtual_ref), custom_call_target="tpu_custom_call" | custom-call | tf_op jit(solution)/shard_map/pallas_call | solution.py:355
  117.1 1.6 %copy.9 = f32[32,1152]{1,0:T(8,128)} copy(f32[32,1152]{1,0:T(8,128)} %shard_map.73) | data formatting | bytes 294912

commit v3 on v2

--- a/solution.py
+++ b/solution.py
@@ -13,9 +13,9 @@
 HALF = 576
 NCOL, NV, NO, NB = 1152, 384, 64, 18
 
-Y_STREAMS = ((0, 256), (512, 512))
-Z_STREAMS = ((256, 256), (1024, 128))
-Y_PIECES = (3, 3)
+Y_STREAMS = ((0, 384), (512, 256), (768, 128))
+Z_STREAMS = ((384, 128), (896, 256))
+Y_PIECES = (3, 3, 1)
 
 
 def split_hi_lo(value):
@@ -37,14 +37,13 @@
 
 def kernel(
     a_hbm, b_ref, integrals_hbm, pairs_ref, window_ref, occupied_ref, virtual_ref, out_ref,
-    a_vmem, integrals, a_hi, a_lo, gathered, b_hi, b_lo, result,
-    yc0, yc1, yb0, yb1, zc0, zc1, zup0, zup1, zdn0, zdn1,
-    wup0, wup1, wdn0, wdn1, ub0, ub1,
-    l_sem, g_send, g_recv, y_send0, y_recv0, y_send1, y_recv1, z_send, z_recv, w_send, w_recv, u_send, u_recv,
+    a_vmem, integrals, a_hi, a_lo, gathered, b_hi, b_lo, result, gaps,
+    yc0, yc1, yc2, yb0, yb1, yb2, zc0, zc1, zup0, zup1, zdn0, zdn1, wb0, wb1, wb2, ub0, ub1,
+    l_sem, g_send, g_recv, ys0, yr0, ys1, yr1, ys2, yr2, z_send, z_recv, w_send, w_recv, u_send, u_recv,
 ):
-    ycs, ybs, y_sends, y_recvs = (yc0, yc1), (yb0, yb1), (y_send0, y_send1), (y_recv0, y_recv1)
-    zcs, zbufs = (zc0, zc1), ((zup0, zdn0), (zup1, zdn1))
-    wbufs, ubs = ((wup0, wdn0), (wup1, wdn1)), (ub0, ub1)
+    ycs, ybs, wbs = (yc0, yc1, yc2), (yb0, yb1, yb2), (wb0, wb1, wb2)
+    y_sends, y_recvs = (ys0, ys1, ys2), (yr0, yr1, yr2)
+    zcs, zbufs, ubs = (zc0, zc1), ((zup0, zdn0), (zup1, zdn1)), (ub0, ub1)
 
     row, col = lax.axis_index("row"), lax.axis_index("col")
     core = lax.rem(row, 2)
@@ -73,6 +72,9 @@
     def at_z(step):
         return device(x, y, lax.rem(z + step + NZ, NZ), core)
 
+    def in_run(dest):
+        return device(x, y, zhi * NL + dest, core)
+
     other_core = device(x, y, z, 1 - core)
 
     def remote(src, dst, send, recv, where):
@@ -87,11 +89,16 @@
     i_copy.start()
 
     barrier = pltpu.get_barrier_semaphore()
-    greeted = [at_x(1), at_x(-1), at_z(1), at_z(-1), at_z(6), other_core]
+    greeted = [at_z(6), at_x(1), at_x(-1), other_core]
     greeted += [at_y(k) for k in range(1, NY)]
+    for dest in range(NL):
+        @pl.when(dest != i)
+        def _():
+            pl.semaphore_signal(barrier, inc=1, device_id=in_run(dest), device_id_type=MESH)
+
     for where in greeted:
         pl.semaphore_signal(barrier, inc=1, device_id=where, device_id_type=MESH)
-    pl.semaphore_wait(barrier, len(greeted))
+    pl.semaphore_wait(barrier, len(greeted) + NL - 1)
 
     events = []
     finish = []
@@ -141,7 +148,7 @@
             b_hi[rows] = hi
             b_lo[rows] = lo
 
-    def multiply(target, first, width):
+    def multiply(target, first, width, k):
         bh, bl = b_hi[first : first + width], b_lo[first : first + width]
 
         def dot(p, q):
@@ -149,12 +156,10 @@
                 p, q, (((1,), (1,)), ((), ())), preferred_element_type=jnp.float32
             )
 
-        @pl.loop(0, NL)
-        def _(k):
-            hi = a_hi[k].reshape(NY * RB, DEPTH)
-            lo = a_lo[k].reshape(NY * RB, DEPTH)
-            value = dot(hi, bh) + (dot(hi, bl) + dot(lo, bh))
-            target[k] = value.reshape(NY, RB, width)
+        hi = a_hi[k].reshape(NY * RB, DEPTH)
+        lo = a_lo[k].reshape(NY * RB, DEPTH)
+        value = dot(hi, bh) + (dot(hi, bl) + dot(lo, bh))
+        target[k] = value.reshape(NY, RB, width)
 
     def y_rows(n, direction, piece):
         size = 3 // Y_PIECES[n]
@@ -172,9 +177,8 @@
             at_y(1 - 2 * direction),
         )
 
-    def y_start(n, piece):
-        for direction in range(2):
-            y_copy(n, direction, 0, piece).start()
+    def y_start(n, direction, piece):
+        y_copy(n, direction, 0, piece).start()
 
     def y_step(n, step, piece):
         for direction in range(2):
@@ -238,10 +242,36 @@
         finish.append(sent)
         return turn, last
 
-    half_rows = [pl.ds(0, RB // 2), pl.ds(RB // 2, RB // 2)]
     half_y = [pl.ds(0, NY // 2), pl.ds(NY // 2, NY // 2)]
     z_lines = [line(zbufs[n], zcs[n], half_y, z_send, z_recv, n) for n in range(2)]
-    w_lines = [line(wbufs[n], ybs[n].at[NY - 2], half_rows, w_send, w_recv, n) for n in range(2)]
+
+    def w_copy(n, dest, source):
+        return remote(
+            ybs[n].at[NY - 2, dest], wbs[n].at[source],
+            w_send.at[n, dest], w_recv.at[n, source], in_run(dest),
+        )
+
+    def w_start(n):
+        for dest in range(NL):
+            @pl.when(dest != i)
+            def _():
+                w_copy(n, dest, i).start()
+
+    def w_last(n):
+        first, width = Y_STREAMS[n]
+        for source in range(NL):
+            @pl.when(source != i)
+            def _():
+                w_copy(n, i, source).wait_recv()
+                ybs[n][NY - 2, i] += wbs[n][source]
+
+        result[:, first : first + width] = ybs[n][NY - 2, i]
+
+    def w_sent(n):
+        for dest in range(NL):
+            @pl.when(dest != i)
+            def _():
+                w_copy(n, dest, i).wait_send()
 
     def u_copy(n, k):
         return remote(
@@ -261,10 +291,17 @@
             total = total + ubs[n][k - 1]
         result[:, first : first + width] = total
 
-    def w_last(n):
-        first, width = Y_STREAMS[n]
-        w_lines[n][1]()
-        result[:, first : first + width] = ybs[n][NY - 2, i]
+    def find_gaps():
+        pairs, window = pairs_ref[...], window_ref[...].reshape(1, NB)
+        occupied, virtual = occupied_ref[...].reshape(1, NO), virtual_ref[...].reshape(1, NV)
+        gap_row = look_up(as_column(pairs[0:1]), virtual) - look_up(as_column(pairs[1:2]), occupied)
+        energy = look_up(as_column(window), virtual)
+        block = lax.broadcasted_iota(jnp.int32, (NB, NCOL), 1) // NO == lax.broadcasted_iota(jnp.int32, (NB, NCOL), 0)
+        energy = jnp.sum(jnp.where(block, jnp.broadcast_to(energy, (NB, NCOL)), 0.0), axis=0, keepdims=True)
+        within = lax.broadcasted_iota(jnp.int32, (NO, NCOL), 1) % NO == lax.broadcasted_iota(jnp.int32, (NO, NCOL), 0)
+        occupied = jnp.broadcast_to(as_column(occupied), (NO, NCOL))
+        gap_col = energy - jnp.sum(jnp.where(within, occupied, 0.0), axis=0, keepdims=True)
+        gaps[...] = gap_row + gap_col
 
     send(b_ref, slot(1, x, core), 0, 0, at_z(6))
     spread(b_ref, 0)
@@ -279,68 +316,77 @@
 
     event(5.0, lambda: collect(0))
     event(8.5, lambda: collect_far(0))
-    event(10.5, lambda: split_b(0))
-    event(11.0, lambda: multiply(ycs[0], *Y_STREAMS[0]))
-    for piece in range(Y_PIECES[0]):
-        event(12.5, lambda piece=piece: y_start(0, piece))
-    event(13.0, lambda: multiply(zcs[0], *Z_STREAMS[0]))
-    event(14.0, lambda: z_lines[0][0](0))
+    event(11.0, lambda: split_b(0))
 
     def pair():
         wait_block(0)
         spread(slot(1, x, core), 1)
 
-    event(15.0, pair)
+    def y_begin(n, when, cost):
+        size = 3 // Y_PIECES[n]
+        for k in range(3):
+            for direction in range(2):
+                event(when, lambda k=3 * direction + k: multiply(ycs[n], *Y_STREAMS[n], k))
+                if (k + 1) % size == 0:
+                    event(when, lambda d=direction, p=k // size: y_start(n, d, p))
+                when += cost
+
+    def y_go(n, when, period):
+        for step in range(NY - 1):
+            for piece in range(Y_PIECES[n]):
+                at = when + period * (step + (piece + 1) / Y_PIECES[n])
+                event(at, lambda step=step, piece=piece: y_step(n, step, piece))
+        event(when + period * (NY - 1) + 0.01, lambda: w_start(n))
+
+    def z_begin(n, when, cost):
+        for k in (5, 0, 4, 1, 3, 2):
+            event(when, lambda k=k: multiply(zcs[n], *Z_STREAMS[n], k))
+            when += cost
+
+    def z_go(n, when, period):
+        for count in range(NL - 1):
+            event(when + period * count, lambda count=count: z_lines[n][0](count))
+        event(when + period * (NL - 1), z_lines[n][1])
+        event(when + period * (NL - 1) + 0.01, lambda: u_start(n))
+
+    y_begin(0, 11.5, 0.5)
+    event(14.7, pair)
+    z_begin(0, 14.8, 0.2)
+    z_go(0, 16.0, 4.2)
+    y_go(0, 14.5, 3.8)
     event(20.0, lambda: collect(1))
     event(23.5, lambda: collect_far(1))
-    event(26.0, lambda: split_b(1))
-    event(26.5, lambda: multiply(ycs[1], *Y_STREAMS[1]))
-    for piece in range(Y_PIECES[1]):
-        event(30.0, lambda piece=piece: y_start(1, piece))
-    event(30.2, lambda: multiply(zcs[1], *Z_STREAMS[1]))
-    event(31.0, lambda: z_lines[1][0](0))
-    for n, begin, period in ((0, 13.0, 2.6), (1, 30.0, 4.3)):
-        for step in range(NY - 1):
-            for piece in range(Y_PIECES[n]):
-                when = begin + period * (step + (piece + 1) / Y_PIECES[n])
-                event(when, lambda n=n, step=step, piece=piece: y_step(n, step, piece))
-    for lines, n, begin, period in (
-        (z_lines, 0, 15.0, 6.5), (z_lines, 1, 31.0, 6.5), (w_lines, 0, 32.0, 5.0), (w_lines, 1, 60.5, 2.6),
-    ):
-        for count in range(0 if lines is w_lines else 1, NL - 1):
-            event(begin + period * count, lambda lines=lines, n=n, count=count: lines[n][0](count))
-    event(47.5, z_lines[0][1])
-    event(47.6, lambda: u_start(0))
-    event(57.0, lambda: w_last(0))
-    event(63.9, z_lines[1][1])
-    event(64.0, lambda: u_start(1))
-    event(72.0, lambda: u_last(0))
-    event(72.1, lambda: u_last(1))
-    event(73.5, lambda: w_last(1))
+    event(27.0, lambda: split_b(1))
+    y_begin(1, 27.5, 0.4)
+    z_begin(1, 30.0, 0.4)
+    z_go(1, 32.5, 6.0)
+    y_begin(2, 33.0, 0.2)
+    y_go(1, 30.0, 4.2)
+    y_go(2, 36.0, 3.7)
+    event(45.0, find_gaps)
+    event(57.0, lambda: u_last(0))
+    event(58.0, lambda: w_last(0))
+    event(75.0, lambda: w_last(1))
+    event(76.0, lambda: w_last(2))
+    event(77.0, lambda: u_last(1))
     for _, _, do in sorted(events, key=lambda e: e[:2]):
         do()
 
     i_copy.wait()
-    pairs = pairs_ref[...]
-    gap_row = look_up(as_column(pairs[0:1]), virtual_ref[...]) - look_up(as_column(pairs[1:2]), occupied_ref[...])
-    energy = look_up(as_column(window_ref[...]), virtual_ref[...])
-    block = lax.broadcasted_iota(jnp.int32, (NB, NCOL), 1) // NO == lax.broadcasted_iota(jnp.int32, (NB, NCOL), 0)
-    energy = jnp.sum(jnp.where(block, jnp.broadcast_to(energy, (NB, NCOL)), 0.0), axis=0, keepdims=True)
-    within = lax.broadcasted_iota(jnp.int32, (NO, NCOL), 1) % NO == lax.broadcasted_iota(jnp.int32, (NO, NCOL), 0)
-    occupied = jnp.broadcast_to(as_column(occupied_ref[...]), (NO, NCOL))
-    gap_col = energy - jnp.sum(jnp.where(within, occupied, 0.0), axis=0, keepdims=True)
     value = result[...]
     turned = jnp.concatenate([value[:, HALF:], value[:, :HALF]], axis=1)
     cycle_term = jnp.where(zhi == 0, value, turned)
-    out_ref[...] = (integrals[...] + cycle_term) / (gap_row + gap_col)
+    out_ref[...] = (integrals[...] + cycle_term) / gaps[...]
 
     for wait in finish:
         wait()
-    for n in range(2):
+    for n in range(len(Y_STREAMS)):
         for direction in range(2):
             for step in range(NY - 1):
                 for piece in range(Y_PIECES[n]):
                     y_copy(n, direction, step, piece).wait_send()
+        w_sent(n)
+    for n in range(len(Z_STREAMS)):
         for k in range(1, NY):
             u_copy(n, k).wait_send()
 
@@ -366,25 +412,22 @@
             vmem((NCOL, DEPTH), bf16),
             vmem((NCOL, DEPTH), bf16),
             vmem((RB, NCOL), f32),
+            vmem((RB, NCOL), f32),
             *[vmem((NL, NY, RB, w), f32) for w in y_widths],
             *[vmem((NY - 1, NL, RB, w), f32) for w in y_widths],
             *[vmem((NL, NY, RB, w), f32) for w in z_widths],
             *[vmem((NL - 1, NY, RB, w), f32) for w in z_widths],
             *[vmem((NL - 1, NY, RB, w), f32) for w in z_widths],
-            *[vmem((NL - 1, RB, w), f32) for w in y_widths],
-            *[vmem((NL - 1, RB, w), f32) for w in y_widths],
+            *[vmem((NL, RB, w), f32) for w in y_widths],
             *[vmem((NY - 1, RB, w), f32) for w in z_widths],
             dma((2,)),
             dma((15,)),
             dma((15,)),
-            dma((2, NY - 1, Y_PIECES[0])),
-            dma((2, NY - 1, Y_PIECES[0])),
-            dma((2, NY - 1, Y_PIECES[1])),
-            dma((2, NY - 1, Y_PIECES[1])),
+            *[dma((2, NY - 1, p)) for p in Y_PIECES for _ in range(2)],
             dma((2, 2, NL - 1, 2)),
             dma((2, 2, NL - 1, 2)),
-            dma((2, 2, NL - 1, 2)),
-            dma((2, 2, NL - 1, 2)),
+            dma((3, NL)),
+            dma((3, NL)),
             dma((2, NY - 1)),
             dma((2, NY - 1)),
         ],
@@ -393,7 +436,7 @@
         ),
     )(
         amplitudes.reshape(NL, NY, RB, DEPTH), intermediates, integrals, row_pairs,
-        window_virtuals.reshape(1, NB), occupied_energies.reshape(1, NO), virtual_energies.reshape(1, NV),
+        window_virtuals, occupied_energies, virtual_energies,
     )
 
 

time: 119 us -> 112 us (0.941)
  the two profiles are of different devices: /device:TPU:2 before, /device:TPU:132 now
where the time goes in v3:
time: 112 us
  Pallas kernels  110 us (98%)
  local copies, waits for them, and re-layouts  1.58 us (1%)
    pallas_call x1, Pallas kernels, on_device(): pl.pallas_call(kernel, out_shape=jax.ShapeDtypeStruct((RB, NCOL), f32), i...  110 us

profile of v3, /device:TPU:132, one launch (start us, length us, event | category | flops | bytes accessed | tf_op | source)
XLA Modules:
  0.0 111.9 jit_solution(3991803207494057957)
XLA Ops:
  0.0 110.3 %shard_map.73 = f32[32,1152]{1,0:T(8,128)} custom-call(f32[6,8,32,512]{3,2,1,0:T(8,128)} %bitcast.1, f32[72,512]{1,0:T(8,128)} %b_ref.1, f32[32,1152]{1,0:T(8,128)} %integrals_hbm.1, s32[2,32]{1,0:T(2,128)} %pairs_ref.1, s32[18]{0:T(128)} %window_ref.1, f32[64]{0:T(128)} %occupied_ref.1, f32[384]{0:T(512)} %virtual_ref.1), custom_call_target="tpu_custom_call" | custom-call | tf_op jit(solution)/shard_map/pallas_call | solution.py:401
  110.3 1.6 %copy.9 = f32[32,1152]{1,0:T(8,128)} copy(f32[32,1152]{1,0:T(8,128)} %shard_map.73) | data formatting | bytes 294912

commit v4 on v3

--- a/solution.py
+++ b/solution.py
@@ -350,7 +350,7 @@
         event(when + period * (NL - 1) + 0.01, lambda: u_start(n))
 
     y_begin(0, 11.5, 0.5)
-    event(14.7, pair)
+    event(11.3, pair)
     z_begin(0, 14.8, 0.2)
     z_go(0, 16.0, 4.2)
     y_go(0, 14.5, 3.8)

time: 112 us -> 115 us (1.027)
  the two profiles are of different devices: /device:TPU:132 before, /device:TPU:64 now
where the time goes in v4:
time: 115 us
  Pallas kernels  114 us (99%)
  local copies, waits for them, and re-layouts  1.58 us (1%)
    pallas_call x1, Pallas kernels, on_device(): pl.pallas_call(kernel, out_shape=jax.ShapeDtypeStruct((RB, NCOL), f32), i...  114 us

profile of v4, /device:TPU:64, one launch (start us, length us, event | category | flops | bytes accessed | tf_op | source)
XLA Modules:
  0.0 115.2 jit_solution(5315409263659043275)
XLA Ops:
  0.0 113.7 %shard_map.73 = f32[32,1152]{1,0:T(8,128)} custom-call(f32[6,8,32,512]{3,2,1,0:T(8,128)} %bitcast.1, f32[72,512]{1,0:T(8,128)} %b_ref.1, f32[32,1152]{1,0:T(8,128)} %integrals_hbm.1, s32[2,32]{1,0:T(2,128)} %pairs_ref.1, s32[18]{0:T(128)} %window_ref.1, f32[64]{0:T(128)} %occupied_ref.1, f32[384]{0:T(512)} %virtual_ref.1), custom_call_target="tpu_custom_call" | custom-call | tf_op jit(solution)/shard_map/pallas_call | solution.py:401
  113.7 1.6 %copy.9 = f32[32,1152]{1,0:T(8,128)} copy(f32[32,1152]{1,0:T(8,128)} %shard_map.73) | data formatting | bytes 294912
